TPU v7x, 512 devices: a whole 4x4x16 slice. The times are simulated.
512 devices in a mesh: section: 32 (over z, x_hi), dp: 4 (over y), mp: 4 (over x_lo, core).
Axes of the slice: x: 4 (x_hi: 2, x_lo: 2; x = x_hi * 2 + x_lo), y: 4, z: 16, core: 2. Of those that a mesh axis runs over, the one named last changes fastest.
Arguments:
- memory: bfloat16 [4, 256, 2048], P('dp', None, ('section', 'mp')), may hold values from -18 to 18
- key_weight: bfloat16 [32, 2048, 2048], P('section', None, 'mp'), may hold values from -1 to 1
- value_weight: bfloat16 [32, 2048, 2048], P('section', None, 'mp'), may hold values from -0.125 to 0.125
- queries: bfloat16 [32, 4, 256, 2048], P('section', 'dp', None, 'mp'), may hold values from -1024 to 1024
- cotangent: bfloat16 [32, 4, 256, 2048], P('section', 'dp', None, 'mp'), may hold values from -6 to 6
- target_lengths: int32 [4], P('dp'), may hold values from 64 to 256, as said below
Outputs:
- context: bfloat16 [32, 4, 256, 2048], P('section', 'dp', None, 'mp')
- mem_grad: float32 [4, 256, 2048], P('dp', None, ('section', 'mp'))
Inputs may be any that keep to these rules, and one draw needn't show every extreme that they name: `target_lengths`: valid positions of a sequence come first; the last sequence is full.
All inputs are finite; a program needn't handle non-finite values.
Results may differ from a plain program's by a relative error of at most 0.013.
The roundings to bfloat16 on the way count: a program that leaves them out, or rounds other values in their place, can miss the bound.
Values may be sent and summed in bfloat16 or wider, within the bound.
No kernel may reach another device: no remote copies, remote signals or barrier semaphores. Data moves between devices by JAX's collectives and lax.ppermute only.
A program may use at most 64 MiB of HBM per device.

v0:
```python
import jax
import jax.numpy as jnp
from jax import lax
from jax.sharding import PartitionSpec as P

HEAD_DIM = 256


def on_device(memory, key_weight, value_weight, queries, cotangent, target_lengths):
    width = key_weight.shape[2]
    head_count = width // HEAD_DIM
    seq_rows = queries.shape[2]
    score_scale = HEAD_DIM ** (-0.5)
    mem_block = memory[0]
    mem_rows = mem_block.shape[0]
    full_memory = lax.all_gather(mem_block, ("section", "mp"), axis=1, tiled=True)
    token_total = lax.psum(target_lengths.astype(jnp.float32), "dp")
    slot_total = float(lax.axis_size("dp") * target_lengths.shape[0] * seq_rows)
    loss_weight = slot_total / token_total[0]
    valid = (jnp.arange(seq_rows, dtype=jnp.int32) < target_lengths[0]).astype(jnp.float32)
    layer_index = 0
    key_rows = jnp.dot(
        full_memory, key_weight[layer_index], preferred_element_type=jnp.float32
    ).astype(jnp.bfloat16)
    value_rows = jnp.dot(
        full_memory, value_weight[layer_index], preferred_element_type=jnp.float32
    ).astype(jnp.bfloat16)
    key_heads = key_rows.reshape(mem_rows, head_count, HEAD_DIM)
    value_heads = value_rows.reshape(mem_rows, head_count, HEAD_DIM)
    query_heads = queries[layer_index, 0].reshape(seq_rows, head_count, HEAD_DIM)
    scores = (
        jnp.einsum("thd,shd->hts", query_heads, key_heads, preferred_element_type=jnp.float32)
        * score_scale
    )
    attention = jax.nn.softmax(scores, axis=-1)
    attention_low = attention.astype(jnp.bfloat16)
    context = jnp.einsum(
        "hts,shd->thd", attention_low, value_heads, preferred_element_type=jnp.float32
    )
    context = (context * valid[:, None, None]).astype(jnp.bfloat16)
    contexts = [context.reshape(seq_rows, width)]
    weighted = cotangent[layer_index, 0].astype(jnp.float32) * (valid * loss_weight)[:, None]
    weighted = weighted.astype(jnp.bfloat16).reshape(seq_rows, head_count, HEAD_DIM)
    value_grad = jnp.einsum(
        "hts,thd->shd", attention_low, weighted, preferred_element_type=jnp.float32
    )
    value_grads = [value_grad.astype(jnp.bfloat16).reshape(mem_rows, width)]
    prob_grad = jnp.einsum(
        "thd,shd->hts", weighted, value_heads, preferred_element_type=jnp.float32
    )
    row_dot = jnp.sum(attention * prob_grad, axis=-1, keepdims=True)
    score_grad = (attention * (prob_grad - row_dot) * score_scale).astype(jnp.bfloat16)
    key_grad = jnp.einsum(
        "hts,thd->shd", score_grad, query_heads, preferred_element_type=jnp.float32
    )
    key_grads = [key_grad.astype(jnp.bfloat16).reshape(mem_rows, width)]
    contract_last = (((1,), (1,)), ((), ()))
    layer_index = 0
    key_part = key_weight[layer_index]
    value_part = value_weight[layer_index]
    running = lax.dot_general(
        key_part, key_grads[layer_index], contract_last, preferred_element_type=jnp.float32
    )
    running = running + lax.dot_general(
        value_part, value_grads[layer_index], contract_last, preferred_element_type=jnp.float32
    )
    own_part = lax.psum_scatter(running, ("section", "mp"), scatter_dimension=0, tiled=True)
    own_grad = own_part.T
    context_out = jnp.stack(contexts, axis=0)[:, None]
    return (context_out, own_grad[None])


def solution(mesh):
    return jax.shard_map(
        on_device,
        mesh=mesh,
        in_specs=(
            P("dp", None, ("section", "mp")),
            P("section", None, "mp"),
            P("section", None, "mp"),
            P("section", "dp", None, "mp"),
            P("section", "dp", None, "mp"),
            P("dp"),
        ),
        out_specs=(P("section", "dp", None, "mp"), P("dp", None, ("section", "mp"))),
        check_vma=False,
    )
```

profile of v0, /device:TPU:8, one launch (start us, length us, event | category | flops | bytes accessed | tf_op | source)
XLA Modules:
  0.0 430.5 jit_solution(5405295528852739863)
XLA Ops:
  7.2 0.7 all-gather.3.cloned.1.call-update
  7.9 0.0 reduce-scatter.4.cloned.1.call-start
  8.6 14.0 %psum.7 = f32[1]{0:T(128)} all-reduce(f32[1]{0:T(128)S(6)} %convert_element_type.59), channel_id=1, replica_groups=mesh['section'=32,'dp'=4,'mp'=4] {'dp'}, use_global_device_ids=true, to_apply=%region_2.0 | all-reduce | flops 1 | bytes 8 | tf_op jit(solution)/shard_map/psum | solution.py:17
  22.6 1.1 copy.41
  23.7 1.2 copy.38
  25.6 120.8 %all-gather.3.cloned.1.call-done = bf16[1,256,2048]{1,2,0:T(8,128)(2,1)} async-done(((bf16[1,256,16]{1,2,0:T(8,128)(2,1)}), bf16[1,256,2048]{1,2,0:T(8,128)(2,1)}) %all-gather.3.cloned.1.call-update) | async-done | bytes 1048592 | tf_op jit(solution)/shard_map/all_gather | solution.py:16
  146.4 1.9 fusion.22
  148.4 1.1 fusion.58
  149.5 2.6 fusion.19
  152.2 0.2 fusion.33
  152.4 0.5 copy-done.4
  152.9 1.6 convolution_convert_fusion
  154.5 1.6 fusion.18
  156.1 0.8 fusion.3
  156.9 0.8 copy-done.1
  157.7 2.1 fusion.2
  159.8 2.9 copy.39
  162.8 0.9 copy-done.3
  163.7 0.1 copy-done.5
  163.8 1.5 fusion.25
  165.3 0.8 copy.32
  166.2 256.0 %reduce-scatter.4.cloned.1.call-done = f32[16,256]{1,0:T(8,128)} async-done(((f32[2048,256]{1,0:T(8,128)}), f32[16,256]{1,0:T(8,128)}) %reduce-scatter.4.cloned.1.call-update) | async-done | bytes 16400
  422.2 0.8 copy.40
  423.0 0.7 copy.33
  (14 shorter events, 0.1 us)
Async XLA Ops:
  7.2 139.3 %copy-start = (bf16[1,2048,512]{2,1,0:T(8,128)(2,1)S(1)}, bf16[1,2048,512]{2,1,0:T(8,128)(2,1)}, u32[]{:S(2)}) copy-start(bf16[1,2048,512]{2,1,0:T(8,128)(2,1)} %param.7) | copy-start | bytes 6291460
  7.2 139.2 %all-gather.3.cloned.1.call-start = ((), (), s32[]{:S(2)}) async-start(), calls=%async_computation.1 | async-start | bytes 1056768 | tf_op jit(solution)/shard_map/all_gather | solution.py:16
  7.9 414.3 %reduce-scatter.4.cloned.1.call-start = ((), (), s32[]{:S(2)}) async-start(), calls=%async_computation.2 | async-start | bytes 2113536
  23.7 124.7 %copy-start.2 = (bf16[1,1,256,512]{2,3,1,0:T(8,128)(2,1)}, bf16[1,1,256,512]{2,3,1,0:T(8,128)(2,1)S(1)}, u32[]{:S(2)}) copy-start(bf16[1,1,256,512]{2,3,1,0:T(8,128)(2,1)S(1)} %copy.41) | copy-start | bytes 786436
  148.4 3.8 copy-start.6
  152.2 0.7 copy-start.4
  156.1 1.6 copy-start.1
  162.7 0.9 copy-start.3
  162.8 1.0 copy-start.5
Sparse Core Ops, SparseCore 0:
  11.0 135.4 all-gather.2
  162.9 259.2 reduce-scatter.3
where the time goes:
time: 431 us
  waiting for transfers between devices  378 us (88%)
  between operations  15.5 us (4%)
  blocking collectives  14 us (3%)
  matrix products  13.5 us (3%)
  local copies, waits for them, and re-layouts  9.84 us (2%)
    unnamed x3, waiting for transfers between devices  257 us
    all_gather x1, waiting for transfers between devices, on_device(): lax.all_gather(mem_block, ('section', 'mp'), axis=1, tiled=True)  121 us
    psum x1, blocking collectives, on_device(): token_total = lax.psum(target_lengths.astype(jnp.float32), 'dp')  14 us
  transfers between devices with their start and end apart: 2, of which 2 were waited for; matrix products, arithmetic and copies ran while one was open for 1% of the time, Pallas kernels for 0%

commit v1 on v0

--- a/solution.py
+++ b/solution.py
@@ -13,7 +13,12 @@
     score_scale = HEAD_DIM ** (-0.5)
     mem_block = memory[0]
     mem_rows = mem_block.shape[0]
-    full_memory = lax.all_gather(mem_block, ("section", "mp"), axis=1, tiled=True)
+    full_memory = jnp.concatenate(
+        lax.all_to_all(
+            jnp.stack([mem_block] * lax.axis_size(("section", "mp"))), ("section", "mp"), 0, 0
+        ),
+        axis=1,
+    )
     token_total = lax.psum(target_lengths.astype(jnp.float32), "dp")
     slot_total = float(lax.axis_size("dp") * target_lengths.shape[0] * seq_rows)
     loss_weight = slot_total / token_total[0]

time: 431 us -> 364 us (0.84)
  waiting for transfers between devices: 378 us -> 296 us
  starting transfers between devices: 0.08 us -> 20.4 us
  blocking collectives: 14 us -> 9.21 us
    all_gather x1 -> x0, waiting for transfers between devices: 121 us -> none  [on_device(): lax.all_gather(mem_block, ('section', 'mp'), axis=1, tiled=True)]
    all_to_all x0 -> x1, waiting for transfers between devices: none -> 41.9 us  [on_device(): lax.all_to_all(jnp.stack([mem_block] * lax.axis_size(('section', 'mp'))),...]
    all_to_all x0 -> x1, starting transfers between devices: none -> 20.3 us  [on_device(): lax.all_to_all(jnp.stack([mem_block] * lax.axis_size(('section', 'mp'))),...]
    psum x1, blocking collectives: 14 us -> 9.21 us  [on_device(): token_total = lax.psum(target_lengths.astype(jnp.float32), 'dp')]
    unnamed x3 -> x2, waiting for transfers between devices: 257 us -> 254 us
where the time goes in v1:
time: 364 us; the launch traced here: 363 us
  waiting for transfers between devices  296 us (81%)
  starting transfers between devices  20.4 us (6%)
  between operations  15.6 us (4%)
  matrix products  13.1 us (4%)
  local copies, waits for them, and re-layouts  9.34 us (3%)
  blocking collectives  9.21 us (3%)
    unnamed x2, waiting for transfers between devices  254 us
    all_to_all x1, waiting for transfers between devices, on_device(): lax.all_to_all(jnp.stack([mem_block] * lax.axis_size(('section', 'mp'))),...  41.9 us
    all_to_all x1, starting transfers between devices, on_device(): lax.all_to_all(jnp.stack([mem_block] * lax.axis_size(('section', 'mp'))),...  20.3 us
    psum x1, blocking collectives, on_device(): token_total = lax.psum(target_lengths.astype(jnp.float32), 'dp')  9.21 us
  transfers between devices with their start and end apart: 2, of which 2 were waited for; matrix products, arithmetic and copies ran while one was open for 1% of the time, Pallas kernels for 0%

profile of v1, /device:TPU:8, one launch (start us, length us, event | category | flops | bytes accessed | tf_op | source)
XLA Modules:
  0.0 363.1 jit_solution(3804488249603954803)
XLA Ops:
  7.2 1.9 stack.3
  9.1 20.3 %all-to-all-start = ((bf16[128,256,16]{1,2,0:T(8,128)(2,1)}), bf16[128,256,16]{1,2,0:T(8,128)(2,1)}, u32[]{:S(2)}, u32[]{:S(2)}) async-start(bf16[128,256,16]{1,2,0:T(8,128)(2,1)} %stack.3), calls=%async_computation | async-start | bytes 2097152 | tf_op jit(solution)/shard_map/all_to_all | solution.py:17
  29.5 0.0 reduce-scatter.4.cloned.1.call-start
  30.2 9.2 %psum.7 = f32[1]{0:T(128)} all-reduce(f32[1]{0:T(128)S(6)} %convert_element_type.59), channel_id=1, replica_groups=mesh['section'=32,'dp'=4,'mp'=4] {'dp'}, use_global_device_ids=true, to_apply=%region_2.0 | all-reduce | flops 1 | bytes 8 | tf_op jit(solution)/shard_map/psum | solution.py:22
  39.4 0.1 copy.55
  39.5 0.1 copy.52
  40.4 41.9 %all-to-all-done = bf16[128,256,16]{1,2,0:T(8,128)(2,1)} async-done(((bf16[128,256,16]{1,2,0:T(8,128)(2,1)}), bf16[128,256,16]{1,2,0:T(8,128)(2,1)}, u32[]{:S(2)}, u32[]{:S(2)}) %all-to-all-start) | async-done | bytes 1048608 | tf_op jit(solution)/shard_map/all_to_all | solution.py:17
  82.3 2.1 fusion.22
  84.4 2.0 fusion.19
  86.5 1.1 fusion.56
  87.6 0.2 fusion.31
  87.8 1.6 convolution_convert_fusion
  89.5 1.6 fusion.18
  91.1 0.8 fusion.3
  91.8 0.8 copy-done.2
  92.7 2.1 fusion.2
  94.7 2.9 copy.53
  97.7 0.9 copy-done.6
  98.6 0.1 copy-done.8
  98.7 1.5 fusion.25
  100.2 0.8 copy.46
  101.1 253.7 %reduce-scatter.4.cloned.1.call-done = f32[16,256]{1,0:T(8,128)} async-done(((f32[2048,256]{1,0:T(8,128)}), f32[16,256]{1,0:T(8,128)}) %reduce-scatter.4.cloned.1.call-update) | async-done | bytes 16400
  354.8 0.8 copy.54
  355.6 0.7 copy.47
  (20 shorter events, 0.1 us)
Async XLA Ops:
  7.2 75.1 %copy-start = (bf16[1,2048,512]{2,1,0:T(8,128)(2,1)S(1)}, bf16[1,2048,512]{2,1,0:T(8,128)(2,1)}, u32[]{:S(2)}) copy-start(bf16[1,2048,512]{2,1,0:T(8,128)(2,1)} %param.7) | copy-start | bytes 6291460
  7.2 32.2 %copy-start.4 = (bf16[1,1,256,512]{3,2,1,0:T(8,128)(2,1)S(1)}, bf16[1,1,256,512]{3,2,1,0:T(8,128)(2,1)}, u32[]{:S(2)}) copy-start(bf16[1,1,256,512]{3,2,1,0:T(8,128)(2,1)} %param.9) | copy-start | bytes 786436
  7.2 32.3 %copy-start.3 = (bf16[1,1,256,512]{3,2,1,0:T(8,128)(2,1)S(1)}, bf16[1,1,256,512]{3,2,1,0:T(8,128)(2,1)}, u32[]{:S(2)}) copy-start(bf16[1,1,256,512]{3,2,1,0:T(8,128)(2,1)} %param.10) | copy-start | bytes 786436
  9.1 73.1 %all-to-all-start = ((bf16[128,256,16]{1,2,0:T(8,128)(2,1)}), bf16[128,256,16]{1,2,0:T(8,128)(2,1)}, u32[]{:S(2)}, u32[]{:S(2)}) async-start(bf16[128,256,16]{1,2,0:T(8,128)(2,1)} %stack.3), calls=%async_computation | async-start | bytes 2097152 | tf_op jit(solution)/shard_map/all_to_all | solution.py:17
  29.5 325.3 %reduce-scatter.4.cloned.1.call-start = ((), (), s32[]{:S(2)}) async-start(), calls=%async_computation.2 | async-start | bytes 2113536
  39.5 46.9 %copy-start.5 = (bf16[1,1,256,512]{2,3,1,0:T(8,128)(2,1)}, bf16[1,1,256,512]{2,3,1,0:T(8,128)(2,1)S(1)}, u32[]{:S(2)}) copy-start(bf16[1,1,256,512]{2,3,1,0:T(8,128)(2,1)S(1)} %copy.55) | copy-start | bytes 786436
  82.3 2.1 copy-start.1
  84.4 3.2 copy-start.9
  86.4 1.4 copy-start.7
  91.1 1.6 copy-start.2
  97.7 0.9 copy-start.6
  97.7 1.0 copy-start.8
Sparse Core Ops, SparseCore 0:
  97.8 256.8 reduce-scatter.3
